TPU v7x, 256 devices: a whole 4x4x8 slice. The times are simulated.
256 devices in a mesh: ctx: 16 (over z, core), row: 4 (over y), col: 4 (over x).
Axes of the slice: x: 4, y: 4, z: 8, core: 2. Of those that a mesh axis runs over, the one named last changes fastest.
Arguments:
- output_grad: bfloat16 [8192, 8192], P('ctx', ('row', 'col')), may hold values from -6 to 6
- conv_out: bfloat16 [8192, 8192], P('ctx', ('row', 'col')), may hold values from -9 to 9
- input_mix: bfloat16 [8192, 4, 256], P('ctx'), may hold values from -0.15625 to 0.15625
- output_mix: bfloat16 [8192, 4, 256], P('ctx'), may hold values from -1 to 1
- step_size: float32 [128, 8192], P(('row', 'col'), 'ctx'), may hold values from 0.5 to 2
- log_decay: float32 [128, 8192], P(('row', 'col'), 'ctx'), may hold values from -2.1 to 0, as said below
- skip_gain: float32 [128], P(('row', 'col')), may hold values from 0.5 to 2
- conv_weight: float32 [4, 8192], P(None, ('row', 'col')), may hold values from -3 to 3
- later_grad: float32 [128, 64, 256], P(('row', 'col')), may hold values from -32 to 32
- proj_weight: bfloat16 [8192, 8192], P('col', 'row'), may hold values from -0.0625 to 0.0625
Outputs:
- hidden_grad: bfloat16 [8192, 8192], P('ctx', ('col', 'row'))
- x_grad: bfloat16 [8192, 8192], P('ctx', ('row', 'col'))
- state_grad: float32 [16, 128, 64, 256], P('ctx', ('row', 'col'))
Inputs may be any that keep to these rules, and one draw needn't show every extreme that they name: `log_decay`: the forward pass's log decay of each head at each token.
All inputs are finite; a program needn't handle non-finite values.
Results may differ from a plain program's by a relative error of at most 0.022.
Values may be sent and summed in bfloat16 or wider, within the bound.
No kernel may reach another device: no remote copies, remote signals or barrier semaphores. Data moves between devices by JAX's collectives and lax.ppermute only.
A program may use at most 128 MiB of HBM per device.

v0:
```python
import jax
import jax.numpy as jnp
from jax import lax
from jax.sharding import PartitionSpec as P

HD = 64
HPG = 32
KW = 4


def from_behind(value, axis, steps):
    count = lax.axis_size(axis)
    first, last = (max(0, -steps), min(count, count - steps))
    return lax.ppermute(value, axis, [(source, source + steps) for source in range(first, last)])


def on_device(
    output_grad,
    conv_out,
    input_mix,
    output_mix,
    step_size,
    log_decay,
    skip_gain,
    conv_weight,
    later_grad,
    proj_weight,
):
    tokens_dev = output_grad.shape[0]
    heads_dev = step_size.shape[0]
    head_block = lax.axis_index("row") * lax.axis_size("col") + lax.axis_index("col")
    group = head_block * heads_dev // HPG
    write_rows = lax.dynamic_index_in_dim(input_mix, group, 1, keepdims=False)
    read_rows = lax.dynamic_index_in_dim(output_mix, group, 1, keepdims=False)
    cumulative = jnp.cumsum(log_decay, axis=1)
    block_end = cumulative[:, -1]
    decays = jnp.exp(block_end)
    per_head = output_grad.reshape(tokens_dev, heads_dev, HD)
    weighted = (jnp.exp(cumulative).T[:, :, None] * per_head.astype(jnp.float32)).astype(
        jnp.bfloat16
    )
    block_sum = jnp.einsum("shd,sn->hdn", weighted, read_rows, preferred_element_type=jnp.float32)
    is_last = lax.axis_index("ctx") == lax.axis_size("ctx") - 1

    def chain_turn(turn_index, estimate):
        passed = from_behind(
            (block_sum + decays[:, None, None] * estimate).astype(jnp.bfloat16), "ctx", -1
        ).astype(jnp.float32)
        return jnp.where(is_last, later_grad, passed)

    carried = lax.fori_loop(
        0,
        lax.axis_size("ctx") - 1,
        chain_turn,
        jnp.where(is_last, later_grad, jnp.zeros_like(later_grad)),
    )
    state_start = block_sum + decays[:, None, None] * carried
    scores = jnp.dot(write_rows, read_rows.T, preferred_element_type=jnp.float32)
    positions = jnp.arange(tokens_dev)
    causal = positions[None, :] >= positions[:, None]
    offsets = cumulative[:, None, :] - cumulative[:, :, None]
    mixing = (jnp.exp(jnp.where(causal[None], offsets, -jnp.inf)) * scores[None]).astype(
        jnp.bfloat16
    )
    intra = jnp.einsum("hts,shd->thd", mixing, per_head, preferred_element_type=jnp.float32)
    inter = jnp.einsum(
        "hdn,tn->thd", carried, write_rows.astype(jnp.float32), precision=lax.Precision.HIGHEST
    )
    inter = inter * jnp.exp(block_end[:, None] - cumulative).T[:, :, None]
    input_grad = step_size.T[:, :, None] * (intra + inter) + skip_gain[
        None, :, None
    ] * per_head.astype(jnp.float32)
    flat_grad = input_grad.reshape(tokens_dev, heads_dev * HD)
    activated = conv_out.astype(jnp.float32)
    sigma = jax.nn.sigmoid(activated)
    pre_grad = (flat_grad * sigma * (1.0 + activated * (1.0 - sigma))).astype(jnp.bfloat16)
    rim_rows = from_behind(pre_grad[: KW - 1], "ctx", -1)
    extended = jnp.concatenate([pre_grad, rim_rows], axis=0).astype(jnp.float32)
    accum = jnp.zeros(pre_grad.shape, jnp.float32)
    for tap in range(KW):
        accum = accum + conv_weight[tap][None, :] * extended[tap : tap + tokens_dev]
    x_grad = accum.astype(jnp.bfloat16)
    partial_grad = lax.dot_general(
        lax.all_gather(x_grad, "col", axis=1, tiled=True),
        proj_weight,
        (((1,), (1,)), ((), ())),
        preferred_element_type=jnp.float32,
    )
    hidden_grad = lax.psum_scatter(
        partial_grad.astype(jnp.bfloat16), "row", scatter_dimension=1, tiled=True
    )
    return (hidden_grad, x_grad, state_start[None])


def solution(mesh):
    return jax.shard_map(
        on_device,
        mesh=mesh,
        in_specs=(
            P("ctx", ("row", "col")),
            P("ctx", ("row", "col")),
            P("ctx", None, None),
            P("ctx", None, None),
            P(("row", "col"), "ctx"),
            P(("row", "col"), "ctx"),
            P(("row", "col")),
            P(None, ("row", "col")),
            P(("row", "col"), None, None),
            P("col", "row"),
        ),
        out_specs=(
            P("ctx", ("col", "row")),
            P("ctx", ("row", "col")),
            P("ctx", ("row", "col"), None, None),
        ),
        check_vma=False,
    )
```

profile of v0, /device:TPU:1, one launch (start us, length us, event | category | flops | bytes accessed | tf_op | source)
XLA Modules:
  0.0 251.9 jit_solution(11634387616972478772)
XLA Ops:
  7.2 2.3 reduce-window.6
  11.5 2.6 %constant_dynamic-slice_fusion = (bf16[512,1,256]{2,1,0:T(2,128)(2,1)S(1)}, bf16[512,1,256]{2,1,0:T(2,128)(2,1)S(1)}) fusion(bf16[512,4,256]{2,1,0:T(4,128)(2,1)} %param.15, s32[]{:T(128)S(6)} %select_n.30, bf16[512,4,256]{2,1,0:T(4,128)(2,1)} %param.14), kind=kLoop, calls=%fused_computation.48 | loop fusion | bytes 1048580 | tf_op jit(solution)/shard_map/jit(dynamic_index_in_dim)/dynamic_slice | solution.py:34
  15.8 4.3 %fusion.2 = f32[512,8,64]{0,2,1:T(8,128)} fusion(bf16[512,8,64]{0,2,1:T(8,128)(2,1)S(1)} %bitcast.41, f32[512,512]{1,0:T(8,128)} %fusion.20, f32[8,512]{1,0:T(8,128)S(1)} %get-tuple-element.49, pred[512,512]{1,0:T(8,128)(4,1)S(1)} %iota_compare_fusion), kind=kOutput, calls=%fused_computation.6 | convolution fusion | flops 276824064 | bytes 2899968 | tf_op jit(solution)/shard_map/hts,shd->thd/dot_general | solution.py:65
  20.1 119.6 %while.10 = (s32[]{:T(128)}, f32[8,64,256]{2,1,0:T(8,128)S(1)}, pred[]{:T(512)}, f32[8]{0:T(128)S(1)}, f32[8,64,256]{2,1,0:T(8,128)S(1)}, /*index=5*/f32[8,64,256]{2,1,0:T(8,128)S(1)}, s32[]{:T(128)}) while((s32[]{:T(128)}, f32[8,64,256]{2,1,0:T(8,128)S(1)}, pred[]{:T(512)}, f32[8]{0:T(128)S(1)}, f32[8,64,256]{2,1,0:T(8,128)S(1)}, ...), condition=%wide.region_3.4_spmd, body=%wide.region_2.3_spmd.sunk | while | flops 655362 | bytes 3670166 | solution.py:51
  20.2 5.2 %collective-permute-start = (bf16[8,64,256]{2,1,0:T(8,128)(2,1)S(1)}, bf16[8,64,256]{2,1,0:T(8,128)(2,1)S(1)}, u32[]{:S(2)}, u32[]{:S(2)}) collective-permute-start(bf16[8,64,256]{2,1,0:T(8,128)(2,1)S(1)} %add_convert_fusion.2), channel_id=1, source_target_pairs={{16,0},{32,16},{48,32},{64,48},{80,64},{96,80},{112,96},{128,112},... | collective-permute-start | bytes 786440 | tf_op jit(solution)/shard_map/while/body/eval_jaxpr/ppermute | solution.py:14
  25.4 3.8 %collective-permute-done = bf16[8,64,256]{2,1,0:T(8,128)(2,1)S(1)} collective-permute-done((bf16[8,64,256]{2,1,0:T(8,128)(2,1)S(1)}, bf16[8,64,256]{2,1,0:T(8,128)(2,1)S(1)}, u32[]{:S(2)}, u32[]{:S(2)}) %collective-permute-start) | collective-permute-done | bytes 262176 | tf_op jit(solution)/shard_map/while/body/eval_jaxpr/ppermute | solution.py:14
  29.4 1.9 collective-permute-start
  31.3 5.8 %collective-permute-done = bf16[8,64,256]{2,1,0:T(8,128)(2,1)S(1)} collective-permute-done((bf16[8,64,256]{2,1,0:T(8,128)(2,1)S(1)}, bf16[8,64,256]{2,1,0:T(8,128)(2,1)S(1)}, u32[]{:S(2)}, u32[]{:S(2)}) %collective-permute-start) | collective-permute-done | bytes 262176 | tf_op jit(solution)/shard_map/while/body/eval_jaxpr/ppermute | solution.py:14
  37.3 1.9 collective-permute-start
  39.2 5.8 %collective-permute-done = bf16[8,64,256]{2,1,0:T(8,128)(2,1)S(1)} collective-permute-done((bf16[8,64,256]{2,1,0:T(8,128)(2,1)S(1)}, bf16[8,64,256]{2,1,0:T(8,128)(2,1)S(1)}, u32[]{:S(2)}, u32[]{:S(2)}) %collective-permute-start) | collective-permute-done | bytes 262176 | tf_op jit(solution)/shard_map/while/body/eval_jaxpr/ppermute | solution.py:14
  45.2 1.9 collective-permute-start
  47.1 5.8 %collective-permute-done = bf16[8,64,256]{2,1,0:T(8,128)(2,1)S(1)} collective-permute-done((bf16[8,64,256]{2,1,0:T(8,128)(2,1)S(1)}, bf16[8,64,256]{2,1,0:T(8,128)(2,1)S(1)}, u32[]{:S(2)}, u32[]{:S(2)}) %collective-permute-start) | collective-permute-done | bytes 262176 | tf_op jit(solution)/shard_map/while/body/eval_jaxpr/ppermute | solution.py:14
  55.0 5.8 %collective-permute-done = bf16[8,64,256]{2,1,0:T(8,128)(2,1)S(1)} collective-permute-done((bf16[8,64,256]{2,1,0:T(8,128)(2,1)S(1)}, bf16[8,64,256]{2,1,0:T(8,128)(2,1)S(1)}, u32[]{:S(2)}, u32[]{:S(2)}) %collective-permute-start) | collective-permute-done | bytes 262176 | tf_op jit(solution)/shard_map/while/body/eval_jaxpr/ppermute | solution.py:14
  62.9 5.8 %collective-permute-done = bf16[8,64,256]{2,1,0:T(8,128)(2,1)S(1)} collective-permute-done((bf16[8,64,256]{2,1,0:T(8,128)(2,1)S(1)}, bf16[8,64,256]{2,1,0:T(8,128)(2,1)S(1)}, u32[]{:S(2)}, u32[]{:S(2)}) %collective-permute-start) | collective-permute-done | bytes 262176 | tf_op jit(solution)/shard_map/while/body/eval_jaxpr/ppermute | solution.py:14
  68.8 1.9 collective-permute-start
  70.8 5.8 %collective-permute-done = bf16[8,64,256]{2,1,0:T(8,128)(2,1)S(1)} collective-permute-done((bf16[8,64,256]{2,1,0:T(8,128)(2,1)S(1)}, bf16[8,64,256]{2,1,0:T(8,128)(2,1)S(1)}, u32[]{:S(2)}, u32[]{:S(2)}) %collective-permute-start) | collective-permute-done | bytes 262176 | tf_op jit(solution)/shard_map/while/body/eval_jaxpr/ppermute | solution.py:14
  76.7 1.9 collective-permute-start
  78.6 5.8 %collective-permute-done = bf16[8,64,256]{2,1,0:T(8,128)(2,1)S(1)} collective-permute-done((bf16[8,64,256]{2,1,0:T(8,128)(2,1)S(1)}, bf16[8,64,256]{2,1,0:T(8,128)(2,1)S(1)}, u32[]{:S(2)}, u32[]{:S(2)}) %collective-permute-start) | collective-permute-done | bytes 262176 | tf_op jit(solution)/shard_map/while/body/eval_jaxpr/ppermute | solution.py:14
  84.6 1.9 collective-permute-start
  86.5 5.8 %collective-permute-done = bf16[8,64,256]{2,1,0:T(8,128)(2,1)S(1)} collective-permute-done((bf16[8,64,256]{2,1,0:T(8,128)(2,1)S(1)}, bf16[8,64,256]{2,1,0:T(8,128)(2,1)S(1)}, u32[]{:S(2)}, u32[]{:S(2)}) %collective-permute-start) | collective-permute-done | bytes 262176 | tf_op jit(solution)/shard_map/while/body/eval_jaxpr/ppermute | solution.py:14
  94.4 5.8 %collective-permute-done = bf16[8,64,256]{2,1,0:T(8,128)(2,1)S(1)} collective-permute-done((bf16[8,64,256]{2,1,0:T(8,128)(2,1)S(1)}, bf16[8,64,256]{2,1,0:T(8,128)(2,1)S(1)}, u32[]{:S(2)}, u32[]{:S(2)}) %collective-permute-start) | collective-permute-done | bytes 262176 | tf_op jit(solution)/shard_map/while/body/eval_jaxpr/ppermute | solution.py:14
  102.3 5.8 %collective-permute-done = bf16[8,64,256]{2,1,0:T(8,128)(2,1)S(1)} collective-permute-done((bf16[8,64,256]{2,1,0:T(8,128)(2,1)S(1)}, bf16[8,64,256]{2,1,0:T(8,128)(2,1)S(1)}, u32[]{:S(2)}, u32[]{:S(2)}) %collective-permute-start) | collective-permute-done | bytes 262176 | tf_op jit(solution)/shard_map/while/body/eval_jaxpr/ppermute | solution.py:14
  110.2 5.8 %collective-permute-done = bf16[8,64,256]{2,1,0:T(8,128)(2,1)S(1)} collective-permute-done((bf16[8,64,256]{2,1,0:T(8,128)(2,1)S(1)}, bf16[8,64,256]{2,1,0:T(8,128)(2,1)S(1)}, u32[]{:S(2)}, u32[]{:S(2)}) %collective-permute-start) | collective-permute-done | bytes 262176 | tf_op jit(solution)/shard_map/while/body/eval_jaxpr/ppermute | solution.py:14
  118.1 5.8 %collective-permute-done = bf16[8,64,256]{2,1,0:T(8,128)(2,1)S(1)} collective-permute-done((bf16[8,64,256]{2,1,0:T(8,128)(2,1)S(1)}, bf16[8,64,256]{2,1,0:T(8,128)(2,1)S(1)}, u32[]{:S(2)}, u32[]{:S(2)}) %collective-permute-start) | collective-permute-done | bytes 262176 | tf_op jit(solution)/shard_map/while/body/eval_jaxpr/ppermute | solution.py:14
  126.0 5.8 %collective-permute-done = bf16[8,64,256]{2,1,0:T(8,128)(2,1)S(1)} collective-permute-done((bf16[8,64,256]{2,1,0:T(8,128)(2,1)S(1)}, bf16[8,64,256]{2,1,0:T(8,128)(2,1)S(1)}, u32[]{:S(2)}, u32[]{:S(2)}) %collective-permute-start) | collective-permute-done | bytes 262176 | tf_op jit(solution)/shard_map/while/body/eval_jaxpr/ppermute | solution.py:14
  133.9 5.8 %collective-permute-done = bf16[8,64,256]{2,1,0:T(8,128)(2,1)S(1)} collective-permute-done((bf16[8,64,256]{2,1,0:T(8,128)(2,1)S(1)}, bf16[8,64,256]{2,1,0:T(8,128)(2,1)S(1)}, u32[]{:S(2)}, u32[]{:S(2)}) %collective-permute-start) | collective-permute-done | bytes 262176 | tf_op jit(solution)/shard_map/while/body/eval_jaxpr/ppermute | solution.py:14
  139.7 2.0 fusion.5
  143.5 1.9 collective-permute-start.1
  145.5 3.0 %collective-permute-done.1 = bf16[3,512]{1,0:T(4,128)(2,1)S(1)} collective-permute-done((bf16[3,512]{1,0:T(4,128)(2,1)S(1)}, bf16[3,512]{1,0:T(4,128)(2,1)S(1)}, u32[]{:S(2)}, u32[]{:S(2)}) %collective-permute-start.1) | collective-permute-done | bytes 3104 | tf_op jit(solution)/shard_map/ppermute | solution.py:14
  149.9 52.7 %all-gather.2.cloned.1.call-done = bf16[512,2048]{1,0:T(8,128)(2,1)} async-done(((bf16[512,512]{1,0:T(8,128)(2,1)}), bf16[512,2048]{1,0:T(8,128)(2,1)}) %all-gather.2.cloned.1.call-update) | async-done | bytes 2097168 | tf_op jit(solution)/shard_map/all_gather | solution.py:84
  202.6 9.9 %convolution_convert_fusion = bf16[512,2048]{1,0:T(8,128)(2,1)} fusion(bf16[512,2048]{1,0:T(8,128)(2,1)} %all-gather.2.cloned.1.call-done, bf16[2048,2048]{1,0:T(8,128)(2,1)} %param.21), kind=kOutput, calls=%fused_computation.5 | convolution fusion | flops 4296015872 | bytes 12582912 | tf_op jit(solution)/shard_map/dot_general | solution.py:83
  213.4 31.6 %reduce-scatter.2.cloned.1.call-done = bf16[512,512]{1,0:T(8,128)(2,1)} async-done(((bf16[512,2048]{1,0:T(8,128)(2,1)}), bf16[512,512]{1,0:T(8,128)(2,1)}) %reduce-scatter.2.cloned.1.call-update) | async-done | bytes 524304 | tf_op jit(solution)/shard_map/reduce_scatter | solution.py:89
  (70 shorter events, 25.8 us)
Async XLA Ops:
  7.2 8.6 %copy-start = (f32[8,64,256]{2,1,0:T(8,128)S(1)}, f32[8,64,256]{2,1,0:T(8,128)}, u32[]{:S(2)}) copy-start(f32[8,64,256]{2,1,0:T(8,128)} %param.20) | copy-start | bytes 1572868
  7.2 195.4 %all-gather.2.cloned.1.call-start = ((), (), s32[]{:S(2)}) async-start(), calls=%async_computation.1 | async-start | bytes 2621440 | tf_op jit(solution)/shard_map/all_gather | solution.py:84
  20.1 119.6 %copy-start.1 = (f32[8,512]{1,0:T(8,128)S(1)}, f32[8,512]{1,0:T(8,128)}, u32[]{:S(2)}) copy-start(f32[8,512]{1,0:T(8,128)} %param.16) | copy-start | bytes 49156
  20.1 119.6 %copy-start.3 = (f32[8]{0:T(128)S(1)}, f32[8]{0:T(128)}, u32[]{:S(2)}) copy-start(f32[8]{0:T(128)} %param.18) | copy-start | bytes 100
  20.2 9.0 %collective-permute-start = (bf16[8,64,256]{2,1,0:T(8,128)(2,1)S(1)}, bf16[8,64,256]{2,1,0:T(8,128)(2,1)S(1)}, u32[]{:S(2)}, u32[]{:S(2)}) collective-permute-start(bf16[8,64,256]{2,1,0:T(8,128)(2,1)S(1)} %add_convert_fusion.2), channel_id=1, source_target_pairs={{16,0},{32,16},{48,32},{64,48},{80,64},{96,80},{112,96},{128,112},... | collective-permute-start | bytes 786440 | tf_op jit(solution)/shard_map/while/body/eval_jaxpr/ppermute | solution.py:14
  29.4 7.7 %collective-permute-start = (bf16[8,64,256]{2,1,0:T(8,128)(2,1)S(1)}, bf16[8,64,256]{2,1,0:T(8,128)(2,1)S(1)}, u32[]{:S(2)}, u32[]{:S(2)}) collective-permute-start(bf16[8,64,256]{2,1,0:T(8,128)(2,1)S(1)} %add_convert_fusion.2), channel_id=1, source_target_pairs={{16,0},{32,16},{48,32},{64,48},{80,64},{96,80},{112,96},{128,112},... | collective-permute-start | bytes 786440 | tf_op jit(solution)/shard_map/while/body/eval_jaxpr/ppermute | solution.py:14
  37.3 7.7 %collective-permute-start = (bf16[8,64,256]{2,1,0:T(8,128)(2,1)S(1)}, bf16[8,64,256]{2,1,0:T(8,128)(2,1)S(1)}, u32[]{:S(2)}, u32[]{:S(2)}) collective-permute-start(bf16[8,64,256]{2,1,0:T(8,128)(2,1)S(1)} %add_convert_fusion.2), channel_id=1, source_target_pairs={{16,0},{32,16},{48,32},{64,48},{80,64},{96,80},{112,96},{128,112},... | collective-permute-start | bytes 786440 | tf_op jit(solution)/shard_map/while/body/eval_jaxpr/ppermute | solution.py:14
  45.2 7.7 %collective-permute-start = (bf16[8,64,256]{2,1,0:T(8,128)(2,1)S(1)}, bf16[8,64,256]{2,1,0:T(8,128)(2,1)S(1)}, u32[]{:S(2)}, u32[]{:S(2)}) collective-permute-start(bf16[8,64,256]{2,1,0:T(8,128)(2,1)S(1)} %add_convert_fusion.2), channel_id=1, source_target_pairs={{16,0},{32,16},{48,32},{64,48},{80,64},{96,80},{112,96},{128,112},... | collective-permute-start | bytes 786440 | tf_op jit(solution)/shard_map/while/body/eval_jaxpr/ppermute | solution.py:14
  53.1 7.7 %collective-permute-start = (bf16[8,64,256]{2,1,0:T(8,128)(2,1)S(1)}, bf16[8,64,256]{2,1,0:T(8,128)(2,1)S(1)}, u32[]{:S(2)}, u32[]{:S(2)}) collective-permute-start(bf16[8,64,256]{2,1,0:T(8,128)(2,1)S(1)} %add_convert_fusion.2), channel_id=1, source_target_pairs={{16,0},{32,16},{48,32},{64,48},{80,64},{96,80},{112,96},{128,112},... | collective-permute-start | bytes 786440 | tf_op jit(solution)/shard_map/while/body/eval_jaxpr/ppermute | solution.py:14
  60.9 7.7 %collective-permute-start = (bf16[8,64,256]{2,1,0:T(8,128)(2,1)S(1)}, bf16[8,64,256]{2,1,0:T(8,128)(2,1)S(1)}, u32[]{:S(2)}, u32[]{:S(2)}) collective-permute-start(bf16[8,64,256]{2,1,0:T(8,128)(2,1)S(1)} %add_convert_fusion.2), channel_id=1, source_target_pairs={{16,0},{32,16},{48,32},{64,48},{80,64},{96,80},{112,96},{128,112},... | collective-permute-start | bytes 786440 | tf_op jit(solution)/shard_map/while/body/eval_jaxpr/ppermute | solution.py:14
  68.8 7.7 %collective-permute-start = (bf16[8,64,256]{2,1,0:T(8,128)(2,1)S(1)}, bf16[8,64,256]{2,1,0:T(8,128)(2,1)S(1)}, u32[]{:S(2)}, u32[]{:S(2)}) collective-permute-start(bf16[8,64,256]{2,1,0:T(8,128)(2,1)S(1)} %add_convert_fusion.2), channel_id=1, source_target_pairs={{16,0},{32,16},{48,32},{64,48},{80,64},{96,80},{112,96},{128,112},... | collective-permute-start | bytes 786440 | tf_op jit(solution)/shard_map/while/body/eval_jaxpr/ppermute | solution.py:14
  76.7 7.7 %collective-permute-start = (bf16[8,64,256]{2,1,0:T(8,128)(2,1)S(1)}, bf16[8,64,256]{2,1,0:T(8,128)(2,1)S(1)}, u32[]{:S(2)}, u32[]{:S(2)}) collective-permute-start(bf16[8,64,256]{2,1,0:T(8,128)(2,1)S(1)} %add_convert_fusion.2), channel_id=1, source_target_pairs={{16,0},{32,16},{48,32},{64,48},{80,64},{96,80},{112,96},{128,112},... | collective-permute-start | bytes 786440 | tf_op jit(solution)/shard_map/while/body/eval_jaxpr/ppermute | solution.py:14
  84.6 7.7 %collective-permute-start = (bf16[8,64,256]{2,1,0:T(8,128)(2,1)S(1)}, bf16[8,64,256]{2,1,0:T(8,128)(2,1)S(1)}, u32[]{:S(2)}, u32[]{:S(2)}) collective-permute-start(bf16[8,64,256]{2,1,0:T(8,128)(2,1)S(1)} %add_convert_fusion.2), channel_id=1, source_target_pairs={{16,0},{32,16},{48,32},{64,48},{80,64},{96,80},{112,96},{128,112},... | collective-permute-start | bytes 786440 | tf_op jit(solution)/shard_map/while/body/eval_jaxpr/ppermute | solution.py:14
  92.5 7.7 %collective-permute-start = (bf16[8,64,256]{2,1,0:T(8,128)(2,1)S(1)}, bf16[8,64,256]{2,1,0:T(8,128)(2,1)S(1)}, u32[]{:S(2)}, u32[]{:S(2)}) collective-permute-start(bf16[8,64,256]{2,1,0:T(8,128)(2,1)S(1)} %add_convert_fusion.2), channel_id=1, source_target_pairs={{16,0},{32,16},{48,32},{64,48},{80,64},{96,80},{112,96},{128,112},... | collective-permute-start | bytes 786440 | tf_op jit(solution)/shard_map/while/body/eval_jaxpr/ppermute | solution.py:14
  100.4 7.7 %collective-permute-start = (bf16[8,64,256]{2,1,0:T(8,128)(2,1)S(1)}, bf16[8,64,256]{2,1,0:T(8,128)(2,1)S(1)}, u32[]{:S(2)}, u32[]{:S(2)}) collective-permute-start(bf16[8,64,256]{2,1,0:T(8,128)(2,1)S(1)} %add_convert_fusion.2), channel_id=1, source_target_pairs={{16,0},{32,16},{48,32},{64,48},{80,64},{96,80},{112,96},{128,112},... | collective-permute-start | bytes 786440 | tf_op jit(solution)/shard_map/while/body/eval_jaxpr/ppermute | solution.py:14
  108.3 7.7 %collective-permute-start = (bf16[8,64,256]{2,1,0:T(8,128)(2,1)S(1)}, bf16[8,64,256]{2,1,0:T(8,128)(2,1)S(1)}, u32[]{:S(2)}, u32[]{:S(2)}) collective-permute-start(bf16[8,64,256]{2,1,0:T(8,128)(2,1)S(1)} %add_convert_fusion.2), channel_id=1, source_target_pairs={{16,0},{32,16},{48,32},{64,48},{80,64},{96,80},{112,96},{128,112},... | collective-permute-start | bytes 786440 | tf_op jit(solution)/shard_map/while/body/eval_jaxpr/ppermute | solution.py:14
  116.2 7.7 %collective-permute-start = (bf16[8,64,256]{2,1,0:T(8,128)(2,1)S(1)}, bf16[8,64,256]{2,1,0:T(8,128)(2,1)S(1)}, u32[]{:S(2)}, u32[]{:S(2)}) collective-permute-start(bf16[8,64,256]{2,1,0:T(8,128)(2,1)S(1)} %add_convert_fusion.2), channel_id=1, source_target_pairs={{16,0},{32,16},{48,32},{64,48},{80,64},{96,80},{112,96},{128,112},... | collective-permute-start | bytes 786440 | tf_op jit(solution)/shard_map/while/body/eval_jaxpr/ppermute | solution.py:14
  124.0 7.7 %collective-permute-start = (bf16[8,64,256]{2,1,0:T(8,128)(2,1)S(1)}, bf16[8,64,256]{2,1,0:T(8,128)(2,1)S(1)}, u32[]{:S(2)}, u32[]{:S(2)}) collective-permute-start(bf16[8,64,256]{2,1,0:T(8,128)(2,1)S(1)} %add_convert_fusion.2), channel_id=1, source_target_pairs={{16,0},{32,16},{48,32},{64,48},{80,64},{96,80},{112,96},{128,112},... | collective-permute-start | bytes 786440 | tf_op jit(solution)/shard_map/while/body/eval_jaxpr/ppermute | solution.py:14
  131.9 7.7 %collective-permute-start = (bf16[8,64,256]{2,1,0:T(8,128)(2,1)S(1)}, bf16[8,64,256]{2,1,0:T(8,128)(2,1)S(1)}, u32[]{:S(2)}, u32[]{:S(2)}) collective-permute-start(bf16[8,64,256]{2,1,0:T(8,128)(2,1)S(1)} %add_convert_fusion.2), channel_id=1, source_target_pairs={{16,0},{32,16},{48,32},{64,48},{80,64},{96,80},{112,96},{128,112},... | collective-permute-start | bytes 786440 | tf_op jit(solution)/shard_map/while/body/eval_jaxpr/ppermute | solution.py:14
  139.7 5.7 %copy-start.2 = (f32[4,512]{1,0:T(4,128)S(1)}, f32[4,512]{1,0:T(4,128)}, u32[]{:S(2)}) copy-start(f32[4,512]{1,0:T(4,128)} %param.19) | copy-start | bytes 24580
  143.5 4.9 %collective-permute-start.1 = (bf16[3,512]{1,0:T(4,128)(2,1)S(1)}, bf16[3,512]{1,0:T(4,128)(2,1)S(1)}, u32[]{:S(2)}, u32[]{:S(2)}) collective-permute-start(bf16[3,512]{1,0:T(4,128)(2,1)S(1)} %slice.50), channel_id=1, source_target_pairs={{16,0},{32,16},{48,32},{64,48},{80,64},{96,80},{112,96},{128,112},... | collective-permute-start | bytes 9224 | tf_op jit(solution)/shard_map/ppermute | solution.py:14
  149.8 95.2 %reduce-scatter.2.cloned.1.call-start = ((), (), s32[]{:S(2)}) async-start(), calls=%async_computation.2 | async-start | bytes 2621440 | tf_op jit(solution)/shard_map/reduce_scatter | solution.py:89
Sparse Core Ops, SparseCore 0:
  150.0 52.5 all-gather.1
  212.6 32.3 reduce-scatter.1
where the time goes:
time: 253 us; the launch traced here: 252 us
  waiting for transfers between devices  172 us (68%)
  starting transfers between devices  34 us (13%)
  matrix products  17.7 us (7%)
  between operations  14.2 us (6%)
  other arithmetic  8.98 us (4%)
  local copies, waits for them, and re-layouts  4.6 us (2%)
    ppermute x16, waiting for transfers between devices, from_behind(): lax.ppermute(value, axis, [(source, source + steps) for source in range(f...  87.5 us
    all_gather x1, waiting for transfers between devices, on_device(): lax.all_gather(x_grad, 'col', axis=1, tiled=True)  52.7 us
    ppermute x16, starting transfers between devices, from_behind(): lax.ppermute(value, axis, [(source, source + steps) for source in range(f...  34 us
    reduce_scatter x1, waiting for transfers between devices, on_device(): lax.psum_scatter(partial_grad.astype(jnp.bfloat16), 'row', scatter_dimens...  31.6 us
    dot_general x1, matrix products, on_device(): lax.dot_general(lax.all_gather(x_grad, 'col', axis=1, tiled=True), proj_w...  9.85 us
  transfers between devices with their start and end apart: 18, of which 18 were waited for; matrix products, arithmetic and copies ran while one was open for 0% of the time, Pallas kernels for 0%

commit v1 on v0

--- a/solution.py
+++ b/solution.py
@@ -6,6 +6,11 @@
 HD = 64
 HPG = 32
 KW = 4
+
+
+def gather_from_all(x, axis, dim):
+    copies = jnp.concatenate([x] * lax.axis_size(axis), axis=dim)
+    return lax.all_to_all(copies, axis, dim, dim, tiled=True)
 
 
 def from_behind(value, axis, steps):
@@ -81,7 +86,7 @@
         accum = accum + conv_weight[tap][None, :] * extended[tap : tap + tokens_dev]
     x_grad = accum.astype(jnp.bfloat16)
     partial_grad = lax.dot_general(
-        lax.all_gather(x_grad, "col", axis=1, tiled=True),
+        gather_from_all(x_grad, "col", 1),
         proj_weight,
         (((1,), (1,)), ((), ())),
         preferred_element_type=jnp.float32,

time: 253 us -> 253 us (level)
  waiting for transfers between devices: 172 us -> 136 us
  blocking collectives: 0 us -> 28.3 us
  local copies, waits for them, and re-layouts: 4.6 us -> 12.9 us
    all_gather x1 -> x0, waiting for transfers between devices: 52.7 us -> none  [on_device(): lax.all_gather(x_grad, 'col', axis=1, tiled=True)]
    all_to_all x0 -> x1, blocking collectives: none -> 28.3 us  [gather_from_all(): return lax.all_to_all(copies, axis, dim, dim, tiled=True)]
    reduce_scatter x1, waiting for transfers between devices: 31.6 us -> 46.7 us  [on_device(): lax.psum_scatter(partial_grad.astype(jnp.bfloat16), 'row', scatter_dimens...]
    all_to_all x0 -> x2, local copies, waits for them, and re-layouts: none -> 4.77 us  [gather_from_all(): return lax.all_to_all(copies, axis, dim, dim, tiled=True)]
    unnamed x9 -> x15, local copies, waits for them, and re-layouts: 1.27 us -> 5.17 us
  transfers between devices with their start and end apart: 18 -> 17, of which waited for: 18 -> 17; matrix products, arithmetic and copies ran while one was open for 0% -> 1% of each run, Pallas kernels for 0% -> 0%
where the time goes in v1:
time: 253 us; the launch traced here: 252 us
  waiting for transfers between devices  136 us (54%)
  starting transfers between devices  34 us (13%)
  blocking collectives  28.3 us (11%)
  matrix products  17.8 us (7%)
  between operations  14.2 us (6%)
  local copies, waits for them, and re-layouts  12.9 us (5%)
  other arithmetic  9.07 us (4%)
    ppermute x16, waiting for transfers between devices, from_behind(): lax.ppermute(value, axis, [(source, source + steps) for source in range(f...  88.8 us
    reduce_scatter x1, waiting for transfers between devices, on_device(): lax.psum_scatter(partial_grad.astype(jnp.bfloat16), 'row', scatter_dimens...  46.7 us
    ppermute x16, starting transfers between devices, from_behind(): lax.ppermute(value, axis, [(source, source + steps) for source in range(f...  34 us
    all_to_all x1, blocking collectives, gather_from_all(): return lax.all_to_all(copies, axis, dim, dim, tiled=True)  28.3 us
    dot_general x1, matrix products, on_device(): lax.dot_general(gather_from_all(x_grad, 'col', 1), proj_weight, (((1,), (...  9.93 us
    unnamed x15, local copies, waits for them, and re-layouts  5.17 us
  transfers between devices with their start and end apart: 17, of which 17 were waited for; matrix products, arithmetic and copies ran while one was open for 1% of the time, Pallas kernels for 0%

profile of v1, /device:TPU:1, one launch (start us, length us, event | category | flops | bytes accessed | tf_op | source)
XLA Modules:
  0.0 252.4 jit_solution(12940283608441111208)
XLA Ops:
  7.2 2.2 reduce-window.6
  11.4 2.0 copy.38
  13.6 2.6 %constant_dynamic-slice_fusion = (bf16[512,1,256]{2,1,0:T(2,128)(2,1)S(1)}, bf16[512,1,256]{2,1,0:T(2,128)(2,1)S(1)}) fusion(bf16[512,4,256]{2,1,0:T(4,128)(2,1)} %param.15, s32[]{:T(128)S(6)} %select_n.30, bf16[512,4,256]{2,1,0:T(4,128)(2,1)} %param.14), kind=kLoop, calls=%fused_computation.50 | loop fusion | bytes 1048580 | tf_op jit(solution)/shard_map/jit(dynamic_index_in_dim)/dynamic_slice | solution.py:39
  17.9 4.2 %fusion.2 = f32[512,8,64]{0,2,1:T(8,128)} fusion(bf16[512,8,64]{0,2,1:T(8,128)(2,1)S(1)} %bitcast.47, f32[512,512]{1,0:T(8,128)} %fusion.20, f32[8,512]{1,0:T(8,128)S(1)} %get-tuple-element.52, pred[512,512]{1,0:T(8,128)(4,1)S(1)} %iota_compare_fusion), kind=kOutput, calls=%fused_computation.7 | convolution fusion | flops 276824064 | bytes 2899968 | tf_op jit(solution)/shard_map/hts,shd->thd/dot_general | solution.py:70
  22.2 119.6 %while.10 = (s32[]{:T(128)}, f32[8,64,256]{2,1,0:T(8,128)S(1)}, pred[]{:T(512)}, f32[8]{0:T(128)S(1)}, f32[8,64,256]{2,1,0:T(8,128)S(1)}, /*index=5*/f32[8,64,256]{2,1,0:T(8,128)S(1)}, s32[]{:T(128)}) while((s32[]{:T(128)}, f32[8,64,256]{2,1,0:T(8,128)S(1)}, pred[]{:T(512)}, f32[8]{0:T(128)S(1)}, f32[8,64,256]{2,1,0:T(8,128)S(1)}, ...), condition=%wide.region_3.4_spmd, body=%wide.region_2.3_spmd.sunk | while | flops 655362 | bytes 3670166 | solution.py:56
  22.3 5.2 %collective-permute-start = (bf16[8,64,256]{2,1,0:T(8,128)(2,1)S(1)}, bf16[8,64,256]{2,1,0:T(8,128)(2,1)S(1)}, u32[]{:S(2)}, u32[]{:S(2)}) collective-permute-start(bf16[8,64,256]{2,1,0:T(8,128)(2,1)S(1)} %add_convert_fusion.2), channel_id=1, source_target_pairs={{16,0},{32,16},{48,32},{64,48},{80,64},{96,80},{112,96},{128,112},... | collective-permute-start | bytes 786440 | tf_op jit(solution)/shard_map/while/body/eval_jaxpr/ppermute | solution.py:19
  27.4 3.8 %collective-permute-done = bf16[8,64,256]{2,1,0:T(8,128)(2,1)S(1)} collective-permute-done((bf16[8,64,256]{2,1,0:T(8,128)(2,1)S(1)}, bf16[8,64,256]{2,1,0:T(8,128)(2,1)S(1)}, u32[]{:S(2)}, u32[]{:S(2)}) %collective-permute-start) | collective-permute-done | bytes 262176 | tf_op jit(solution)/shard_map/while/body/eval_jaxpr/ppermute | solution.py:19
  31.5 1.9 collective-permute-start
  33.4 5.8 %collective-permute-done = bf16[8,64,256]{2,1,0:T(8,128)(2,1)S(1)} collective-permute-done((bf16[8,64,256]{2,1,0:T(8,128)(2,1)S(1)}, bf16[8,64,256]{2,1,0:T(8,128)(2,1)S(1)}, u32[]{:S(2)}, u32[]{:S(2)}) %collective-permute-start) | collective-permute-done | bytes 262176 | tf_op jit(solution)/shard_map/while/body/eval_jaxpr/ppermute | solution.py:19
  41.3 5.8 %collective-permute-done = bf16[8,64,256]{2,1,0:T(8,128)(2,1)S(1)} collective-permute-done((bf16[8,64,256]{2,1,0:T(8,128)(2,1)S(1)}, bf16[8,64,256]{2,1,0:T(8,128)(2,1)S(1)}, u32[]{:S(2)}, u32[]{:S(2)}) %collective-permute-start) | collective-permute-done | bytes 262176 | tf_op jit(solution)/shard_map/while/body/eval_jaxpr/ppermute | solution.py:19
  49.2 5.8 %collective-permute-done = bf16[8,64,256]{2,1,0:T(8,128)(2,1)S(1)} collective-permute-done((bf16[8,64,256]{2,1,0:T(8,128)(2,1)S(1)}, bf16[8,64,256]{2,1,0:T(8,128)(2,1)S(1)}, u32[]{:S(2)}, u32[]{:S(2)}) %collective-permute-start) | collective-permute-done | bytes 262176 | tf_op jit(solution)/shard_map/while/body/eval_jaxpr/ppermute | solution.py:19
  57.1 5.8 %collective-permute-done = bf16[8,64,256]{2,1,0:T(8,128)(2,1)S(1)} collective-permute-done((bf16[8,64,256]{2,1,0:T(8,128)(2,1)S(1)}, bf16[8,64,256]{2,1,0:T(8,128)(2,1)S(1)}, u32[]{:S(2)}, u32[]{:S(2)}) %collective-permute-start) | collective-permute-done | bytes 262176 | tf_op jit(solution)/shard_map/while/body/eval_jaxpr/ppermute | solution.py:19
  64.9 5.8 %collective-permute-done = bf16[8,64,256]{2,1,0:T(8,128)(2,1)S(1)} collective-permute-done((bf16[8,64,256]{2,1,0:T(8,128)(2,1)S(1)}, bf16[8,64,256]{2,1,0:T(8,128)(2,1)S(1)}, u32[]{:S(2)}, u32[]{:S(2)}) %collective-permute-start) | collective-permute-done | bytes 262176 | tf_op jit(solution)/shard_map/while/body/eval_jaxpr/ppermute | solution.py:19
  72.8 5.8 %collective-permute-done = bf16[8,64,256]{2,1,0:T(8,128)(2,1)S(1)} collective-permute-done((bf16[8,64,256]{2,1,0:T(8,128)(2,1)S(1)}, bf16[8,64,256]{2,1,0:T(8,128)(2,1)S(1)}, u32[]{:S(2)}, u32[]{:S(2)}) %collective-permute-start) | collective-permute-done | bytes 262176 | tf_op jit(solution)/shard_map/while/body/eval_jaxpr/ppermute | solution.py:19
  80.7 5.8 %collective-permute-done = bf16[8,64,256]{2,1,0:T(8,128)(2,1)S(1)} collective-permute-done((bf16[8,64,256]{2,1,0:T(8,128)(2,1)S(1)}, bf16[8,64,256]{2,1,0:T(8,128)(2,1)S(1)}, u32[]{:S(2)}, u32[]{:S(2)}) %collective-permute-start) | collective-permute-done | bytes 262176 | tf_op jit(solution)/shard_map/while/body/eval_jaxpr/ppermute | solution.py:19
  86.7 1.9 collective-permute-start
  88.6 5.8 %collective-permute-done = bf16[8,64,256]{2,1,0:T(8,128)(2,1)S(1)} collective-permute-done((bf16[8,64,256]{2,1,0:T(8,128)(2,1)S(1)}, bf16[8,64,256]{2,1,0:T(8,128)(2,1)S(1)}, u32[]{:S(2)}, u32[]{:S(2)}) %collective-permute-start) | collective-permute-done | bytes 262176 | tf_op jit(solution)/shard_map/while/body/eval_jaxpr/ppermute | solution.py:19
  94.6 1.9 collective-permute-start
  96.5 5.8 %collective-permute-done = bf16[8,64,256]{2,1,0:T(8,128)(2,1)S(1)} collective-permute-done((bf16[8,64,256]{2,1,0:T(8,128)(2,1)S(1)}, bf16[8,64,256]{2,1,0:T(8,128)(2,1)S(1)}, u32[]{:S(2)}, u32[]{:S(2)}) %collective-permute-start) | collective-permute-done | bytes 262176 | tf_op jit(solution)/shard_map/while/body/eval_jaxpr/ppermute | solution.py:19
  102.4 1.9 collective-permute-start
  104.4 5.8 %collective-permute-done = bf16[8,64,256]{2,1,0:T(8,128)(2,1)S(1)} collective-permute-done((bf16[8,64,256]{2,1,0:T(8,128)(2,1)S(1)}, bf16[8,64,256]{2,1,0:T(8,128)(2,1)S(1)}, u32[]{:S(2)}, u32[]{:S(2)}) %collective-permute-start) | collective-permute-done | bytes 262176 | tf_op jit(solution)/shard_map/while/body/eval_jaxpr/ppermute | solution.py:19
  112.3 5.8 %collective-permute-done = bf16[8,64,256]{2,1,0:T(8,128)(2,1)S(1)} collective-permute-done((bf16[8,64,256]{2,1,0:T(8,128)(2,1)S(1)}, bf16[8,64,256]{2,1,0:T(8,128)(2,1)S(1)}, u32[]{:S(2)}, u32[]{:S(2)}) %collective-permute-start) | collective-permute-done | bytes 262176 | tf_op jit(solution)/shard_map/while/body/eval_jaxpr/ppermute | solution.py:19
  120.1 5.8 %collective-permute-done = bf16[8,64,256]{2,1,0:T(8,128)(2,1)S(1)} collective-permute-done((bf16[8,64,256]{2,1,0:T(8,128)(2,1)S(1)}, bf16[8,64,256]{2,1,0:T(8,128)(2,1)S(1)}, u32[]{:S(2)}, u32[]{:S(2)}) %collective-permute-start) | collective-permute-done | bytes 262176 | tf_op jit(solution)/shard_map/while/body/eval_jaxpr/ppermute | solution.py:19
  128.0 5.8 %collective-permute-done = bf16[8,64,256]{2,1,0:T(8,128)(2,1)S(1)} collective-permute-done((bf16[8,64,256]{2,1,0:T(8,128)(2,1)S(1)}, bf16[8,64,256]{2,1,0:T(8,128)(2,1)S(1)}, u32[]{:S(2)}, u32[]{:S(2)}) %collective-permute-start) | collective-permute-done | bytes 262176 | tf_op jit(solution)/shard_map/while/body/eval_jaxpr/ppermute | solution.py:19
  135.9 5.8 %collective-permute-done = bf16[8,64,256]{2,1,0:T(8,128)(2,1)S(1)} collective-permute-done((bf16[8,64,256]{2,1,0:T(8,128)(2,1)S(1)}, bf16[8,64,256]{2,1,0:T(8,128)(2,1)S(1)}, u32[]{:S(2)}, u32[]{:S(2)}) %collective-permute-start) | collective-permute-done | bytes 262176 | tf_op jit(solution)/shard_map/while/body/eval_jaxpr/ppermute | solution.py:19
  141.8 2.0 fusion.5
  147.2 4.3 %collective-permute-done.1 = bf16[3,512]{0,1:T(8,128)(2,1)S(1)} collective-permute-done((bf16[3,512]{0,1:T(8,128)(2,1)S(1)}, bf16[3,512]{0,1:T(8,128)(2,1)S(1)}, u32[]{:S(2)}, u32[]{:S(2)}) %collective-permute-start.1) | collective-permute-done | bytes 3104 | tf_op jit(solution)/shard_map/ppermute | solution.py:19
  153.9 2.4 copy.39
  156.3 28.3 %all_to_all.12 = bf16[512,4,512]{2,0,1:T(8,128)(2,1)S(1)} all-to-all(bf16[512,4,512]{2,0,1:T(8,128)(2,1)} %copy.39), channel_id=1, replica_groups=mesh['ctx'=16,'row'=4,'col'=4] {'col'}, dimensions={1} | all-to-all | bytes 4194304 | tf_op jit(solution)/shard_map/all_to_all | solution.py:13
  184.6 2.4 copy.40
  187.0 9.9 %convolution_convert_fusion = bf16[512,2048]{1,0:T(8,128)(2,1)} fusion(bf16[512,2048]{0,1:T(8,128)(2,1)} %bitcast.49, bf16[2048,2048]{1,0:T(8,128)(2,1)} %param.21), kind=kOutput, calls=%fused_computation.5 | convolution fusion | flops 4296015872 | bytes 12582912 | tf_op jit(solution)/shard_map/dot_general | solution.py:88
  198.8 46.7 %reduce-scatter.2.cloned.1.call-done = bf16[512,512]{1,0:T(8,128)(2,1)} async-done(((bf16[512,2048]{1,0:T(8,128)(2,1)}), bf16[512,512]{1,0:T(8,128)(2,1)}) %reduce-scatter.2.cloned.1.call-update) | async-done | bytes 524304 | tf_op jit(solution)/shard_map/reduce_scatter | solution.py:94
  (76 shorter events, 33.2 us)
Async XLA Ops:
  7.2 238.4 %reduce-scatter.2.cloned.1.call-start = ((), (), s32[]{:S(2)}) async-start(), calls=%async_computation.2 | async-start | bytes 2621440 | tf_op jit(solution)/shard_map/reduce_scatter | solution.py:94
  10.0 7.9 %copy-start = (f32[8,64,256]{2,1,0:T(8,128)S(1)}, f32[8,64,256]{2,1,0:T(8,128)}, u32[]{:S(2)}) copy-start(f32[8,64,256]{2,1,0:T(8,128)} %param.20) | copy-start | bytes 1572868
  22.2 119.6 %copy-start.3 = (f32[8,512]{1,0:T(8,128)S(1)}, f32[8,512]{1,0:T(8,128)}, u32[]{:S(2)}) copy-start(f32[8,512]{1,0:T(8,128)} %param.16) | copy-start | bytes 49156
  22.2 119.6 %copy-start.5 = (f32[8]{0:T(128)S(1)}, f32[8]{0:T(128)}, u32[]{:S(2)}) copy-start(f32[8]{0:T(128)} %param.18) | copy-start | bytes 100
  22.3 9.0 %collective-permute-start = (bf16[8,64,256]{2,1,0:T(8,128)(2,1)S(1)}, bf16[8,64,256]{2,1,0:T(8,128)(2,1)S(1)}, u32[]{:S(2)}, u32[]{:S(2)}) collective-permute-start(bf16[8,64,256]{2,1,0:T(8,128)(2,1)S(1)} %add_convert_fusion.2), channel_id=1, source_target_pairs={{16,0},{32,16},{48,32},{64,48},{80,64},{96,80},{112,96},{128,112},... | collective-permute-start | bytes 786440 | tf_op jit(solution)/shard_map/while/body/eval_jaxpr/ppermute | solution.py:19
  31.5 7.7 %collective-permute-start = (bf16[8,64,256]{2,1,0:T(8,128)(2,1)S(1)}, bf16[8,64,256]{2,1,0:T(8,128)(2,1)S(1)}, u32[]{:S(2)}, u32[]{:S(2)}) collective-permute-start(bf16[8,64,256]{2,1,0:T(8,128)(2,1)S(1)} %add_convert_fusion.2), channel_id=1, source_target_pairs={{16,0},{32,16},{48,32},{64,48},{80,64},{96,80},{112,96},{128,112},... | collective-permute-start | bytes 786440 | tf_op jit(solution)/shard_map/while/body/eval_jaxpr/ppermute | solution.py:19
  39.4 7.7 %collective-permute-start = (bf16[8,64,256]{2,1,0:T(8,128)(2,1)S(1)}, bf16[8,64,256]{2,1,0:T(8,128)(2,1)S(1)}, u32[]{:S(2)}, u32[]{:S(2)}) collective-permute-start(bf16[8,64,256]{2,1,0:T(8,128)(2,1)S(1)} %add_convert_fusion.2), channel_id=1, source_target_pairs={{16,0},{32,16},{48,32},{64,48},{80,64},{96,80},{112,96},{128,112},... | collective-permute-start | bytes 786440 | tf_op jit(solution)/shard_map/while/body/eval_jaxpr/ppermute | solution.py:19
  47.2 7.7 %collective-permute-start = (bf16[8,64,256]{2,1,0:T(8,128)(2,1)S(1)}, bf16[8,64,256]{2,1,0:T(8,128)(2,1)S(1)}, u32[]{:S(2)}, u32[]{:S(2)}) collective-permute-start(bf16[8,64,256]{2,1,0:T(8,128)(2,1)S(1)} %add_convert_fusion.2), channel_id=1, source_target_pairs={{16,0},{32,16},{48,32},{64,48},{80,64},{96,80},{112,96},{128,112},... | collective-permute-start | bytes 786440 | tf_op jit(solution)/shard_map/while/body/eval_jaxpr/ppermute | solution.py:19
  55.1 7.7 %collective-permute-start = (bf16[8,64,256]{2,1,0:T(8,128)(2,1)S(1)}, bf16[8,64,256]{2,1,0:T(8,128)(2,1)S(1)}, u32[]{:S(2)}, u32[]{:S(2)}) collective-permute-start(bf16[8,64,256]{2,1,0:T(8,128)(2,1)S(1)} %add_convert_fusion.2), channel_id=1, source_target_pairs={{16,0},{32,16},{48,32},{64,48},{80,64},{96,80},{112,96},{128,112},... | collective-permute-start | bytes 786440 | tf_op jit(solution)/shard_map/while/body/eval_jaxpr/ppermute | solution.py:19
  63.0 7.7 %collective-permute-start = (bf16[8,64,256]{2,1,0:T(8,128)(2,1)S(1)}, bf16[8,64,256]{2,1,0:T(8,128)(2,1)S(1)}, u32[]{:S(2)}, u32[]{:S(2)}) collective-permute-start(bf16[8,64,256]{2,1,0:T(8,128)(2,1)S(1)} %add_convert_fusion.2), channel_id=1, source_target_pairs={{16,0},{32,16},{48,32},{64,48},{80,64},{96,80},{112,96},{128,112},... | collective-permute-start | bytes 786440 | tf_op jit(solution)/shard_map/while/body/eval_jaxpr/ppermute | solution.py:19
  70.9 7.7 %collective-permute-start = (bf16[8,64,256]{2,1,0:T(8,128)(2,1)S(1)}, bf16[8,64,256]{2,1,0:T(8,128)(2,1)S(1)}, u32[]{:S(2)}, u32[]{:S(2)}) collective-permute-start(bf16[8,64,256]{2,1,0:T(8,128)(2,1)S(1)} %add_convert_fusion.2), channel_id=1, source_target_pairs={{16,0},{32,16},{48,32},{64,48},{80,64},{96,80},{112,96},{128,112},... | collective-permute-start | bytes 786440 | tf_op jit(solution)/shard_map/while/body/eval_jaxpr/ppermute | solution.py:19
  78.8 7.7 %collective-permute-start = (bf16[8,64,256]{2,1,0:T(8,128)(2,1)S(1)}, bf16[8,64,256]{2,1,0:T(8,128)(2,1)S(1)}, u32[]{:S(2)}, u32[]{:S(2)}) collective-permute-start(bf16[8,64,256]{2,1,0:T(8,128)(2,1)S(1)} %add_convert_fusion.2), channel_id=1, source_target_pairs={{16,0},{32,16},{48,32},{64,48},{80,64},{96,80},{112,96},{128,112},... | collective-permute-start | bytes 786440 | tf_op jit(solution)/shard_map/while/body/eval_jaxpr/ppermute | solution.py:19
  86.7 7.7 %collective-permute-start = (bf16[8,64,256]{2,1,0:T(8,128)(2,1)S(1)}, bf16[8,64,256]{2,1,0:T(8,128)(2,1)S(1)}, u32[]{:S(2)}, u32[]{:S(2)}) collective-permute-start(bf16[8,64,256]{2,1,0:T(8,128)(2,1)S(1)} %add_convert_fusion.2), channel_id=1, source_target_pairs={{16,0},{32,16},{48,32},{64,48},{80,64},{96,80},{112,96},{128,112},... | collective-permute-start | bytes 786440 | tf_op jit(solution)/shard_map/while/body/eval_jaxpr/ppermute | solution.py:19
  94.6 7.7 %collective-permute-start = (bf16[8,64,256]{2,1,0:T(8,128)(2,1)S(1)}, bf16[8,64,256]{2,1,0:T(8,128)(2,1)S(1)}, u32[]{:S(2)}, u32[]{:S(2)}) collective-permute-start(bf16[8,64,256]{2,1,0:T(8,128)(2,1)S(1)} %add_convert_fusion.2), channel_id=1, source_target_pairs={{16,0},{32,16},{48,32},{64,48},{80,64},{96,80},{112,96},{128,112},... | collective-permute-start | bytes 786440 | tf_op jit(solution)/shard_map/while/body/eval_jaxpr/ppermute | solution.py:19
  102.4 7.7 %collective-permute-start = (bf16[8,64,256]{2,1,0:T(8,128)(2,1)S(1)}, bf16[8,64,256]{2,1,0:T(8,128)(2,1)S(1)}, u32[]{:S(2)}, u32[]{:S(2)}) collective-permute-start(bf16[8,64,256]{2,1,0:T(8,128)(2,1)S(1)} %add_convert_fusion.2), channel_id=1, source_target_pairs={{16,0},{32,16},{48,32},{64,48},{80,64},{96,80},{112,96},{128,112},... | collective-permute-start | bytes 786440 | tf_op jit(solution)/shard_map/while/body/eval_jaxpr/ppermute | solution.py:19
  110.3 7.7 %collective-permute-start = (bf16[8,64,256]{2,1,0:T(8,128)(2,1)S(1)}, bf16[8,64,256]{2,1,0:T(8,128)(2,1)S(1)}, u32[]{:S(2)}, u32[]{:S(2)}) collective-permute-start(bf16[8,64,256]{2,1,0:T(8,128)(2,1)S(1)} %add_convert_fusion.2), channel_id=1, source_target_pairs={{16,0},{32,16},{48,32},{64,48},{80,64},{96,80},{112,96},{128,112},... | collective-permute-start | bytes 786440 | tf_op jit(solution)/shard_map/while/body/eval_jaxpr/ppermute | solution.py:19
  118.2 7.7 %collective-permute-start = (bf16[8,64,256]{2,1,0:T(8,128)(2,1)S(1)}, bf16[8,64,256]{2,1,0:T(8,128)(2,1)S(1)}, u32[]{:S(2)}, u32[]{:S(2)}) collective-permute-start(bf16[8,64,256]{2,1,0:T(8,128)(2,1)S(1)} %add_convert_fusion.2), channel_id=1, source_target_pairs={{16,0},{32,16},{48,32},{64,48},{80,64},{96,80},{112,96},{128,112},... | collective-permute-start | bytes 786440 | tf_op jit(solution)/shard_map/while/body/eval_jaxpr/ppermute | solution.py:19
  126.1 7.7 %collective-permute-start = (bf16[8,64,256]{2,1,0:T(8,128)(2,1)S(1)}, bf16[8,64,256]{2,1,0:T(8,128)(2,1)S(1)}, u32[]{:S(2)}, u32[]{:S(2)}) collective-permute-start(bf16[8,64,256]{2,1,0:T(8,128)(2,1)S(1)} %add_convert_fusion.2), channel_id=1, source_target_pairs={{16,0},{32,16},{48,32},{64,48},{80,64},{96,80},{112,96},{128,112},... | collective-permute-start | bytes 786440 | tf_op jit(solution)/shard_map/while/body/eval_jaxpr/ppermute | solution.py:19
  134.0 7.7 %collective-permute-start = (bf16[8,64,256]{2,1,0:T(8,128)(2,1)S(1)}, bf16[8,64,256]{2,1,0:T(8,128)(2,1)S(1)}, u32[]{:S(2)}, u32[]{:S(2)}) collective-permute-start(bf16[8,64,256]{2,1,0:T(8,128)(2,1)S(1)} %add_convert_fusion.2), channel_id=1, source_target_pairs={{16,0},{32,16},{48,32},{64,48},{80,64},{96,80},{112,96},{128,112},... | collective-permute-start | bytes 786440 | tf_op jit(solution)/shard_map/while/body/eval_jaxpr/ppermute | solution.py:19
  141.8 5.4 %copy-start.4 = (f32[4,512]{1,0:T(4,128)S(1)}, f32[4,512]{1,0:T(4,128)}, u32[]{:S(2)}) copy-start(f32[4,512]{1,0:T(4,128)} %param.19) | copy-start | bytes 24580
  145.3 6.3 %collective-permute-start.1 = (bf16[3,512]{0,1:T(8,128)(2,1)S(1)}, bf16[3,512]{0,1:T(8,128)(2,1)S(1)}, u32[]{:S(2)}, u32[]{:S(2)}) collective-permute-start(bf16[3,512]{0,1:T(8,128)(2,1)S(1)} %slice.50), channel_id=1, source_target_pairs={{16,0},{32,16},{48,32},{64,48},{80,64},{96,80},{112,96},{128,112},... | collective-permute-start | bytes 9224 | tf_op jit(solution)/shard_map/ppermute | solution.py:19
  152.9 0.8 copy-start.1
  187.0 10.9 %copy-start.2 = (bf16[512,512]{0,1:T(8,128)(2,1)S(1)}, bf16[512,512]{0,1:T(8,128)(2,1)}, u32[]{:S(2)}) copy-start(bf16[512,512]{0,1:T(8,128)(2,1)} %copy-done.1) | copy-start | bytes 1572868
Sparse Core Ops, SparseCore 0:
  197.0 48.4 reduce-scatter.1
